TPU v7x, 1024 devices: a whole 4x4x32 slice. The times are simulated.
1024 devices in a mesh: ctx: 128 (over z, y), head: 8 (over x, core).
Axes of the slice: x: 4, y: 4, z: 32, core: 2. Of those that a mesh axis runs over, the one named last changes fastest.
Arguments:
- query_self: bfloat16 [8192, 8192], P('ctx', 'head'), may hold values from -60 to 60
- key_self: bfloat16 [8192, 1024], P('ctx', 'head'), may hold values from -6 to 6
- value_self: bfloat16 [8192, 1024], P('ctx', 'head'), may hold values from -6 to 6
- positions: int32 [8192], P('ctx'), may hold values from 0 to 24573, as said below
- query_cross: bfloat16 [8192, 8192], P('ctx', 'head'), may hold values from -60 to 60
- key_vision: bfloat16 [7168, 1024], P('ctx', 'head'), may hold values from -6 to 6
- value_vision: bfloat16 [7168, 1024], P('ctx', 'head'), may hold values from -6 to 6
- media_range: int32 [512, 2], P('ctx'), may hold values from 0 to 8, as said below
- gate_scale: float32 [1], replicated, may hold values from 0.3 to 1.5
Outputs:
- self_context: bfloat16 [8192, 8192], P(('ctx', 'head'))
- cross_context: bfloat16 [8192, 8192], P(('ctx', 'head'))
Inputs may be any that keep to these rules, and one draw needn't show every extreme that they name: `positions`: strictly increasing along the transcript, starting at 0; gaps of 1 to 3 up to the next-to-last token, and the last token's position is exactly 24573. `media_range`: column 0 never exceeds column 1; column 1 never falls from block to block, is 0 for the leading blocks (which see no frame) and 8 for the last block.
All inputs are finite; a program needn't handle non-finite values.
Results may differ from a plain program's by a relative error of at most 0.0091.
Values may be sent and summed in bfloat16 or wider, within the bound.
A program may use at most 32 MiB of HBM per device.

v0:
```python
import jax
import jax.numpy as jnp
from jax import lax
from jax.sharding import PartitionSpec as P

HD = 128
TBLOCK = 16
FRAME_LEN = 896


rope_base = 500000.0
lowest = -1e30


def rotate(values, positions):
    half_width = values.shape[-1] // 2
    exponents = jnp.arange(half_width, dtype=jnp.float32) * (2.0 / values.shape[-1])
    frequency = jnp.power(rope_base, -exponents)
    angles = positions.astype(jnp.float32)[:, None] * frequency[None, :]
    cosine = jnp.cos(angles)[:, None, :]
    sine_part = jnp.sin(angles)[:, None, :]
    first_half = values[..., :half_width]
    second_half = values[..., half_width:]
    return jnp.concatenate(
        [
            first_half * cosine - second_half * sine_part,
            second_half * cosine + first_half * sine_part,
        ],
        axis=-1,
    )


def key_block(key_count):
    block_size = min(key_count, 1024)
    while key_count % block_size != 0:
        block_size = block_size - 1
    return block_size


def attend_block(state_in, queries, key_rows, value_rows, allowed):
    maxima, totals, accumulated = state_in
    scale_factor = queries.shape[-1] ** (-0.5)
    scores = (
        jnp.einsum("rkgd,nkd->kgrn", queries, key_rows, preferred_element_type=jnp.float32)
        * scale_factor
    )
    visible = allowed[None, None, :, :]
    scores = jnp.where(visible, scores, lowest)
    new_maxima = jnp.maximum(maxima, jnp.max(scores, axis=-1))
    weights = jnp.where(visible, jnp.exp(scores - new_maxima[..., None]), 0.0)
    factor = jnp.exp(maxima - new_maxima)
    totals = totals * factor + jnp.sum(weights, axis=-1)
    accumulated = accumulated * factor[..., None] + jnp.einsum(
        "kgrn,nkd->kgrd",
        weights.astype(jnp.bfloat16),
        value_rows,
        preferred_element_type=jnp.float32,
    )
    return (new_maxima, totals, accumulated)


def attend(state_in, queries, key_rows, value_rows, allowed):
    key_count = key_rows.shape[0]
    block_size = key_block(key_count)

    def step_block(block_index, state_now):
        row_begin = block_index * block_size
        key_part = lax.dynamic_slice_in_dim(key_rows, row_begin, block_size, 0)
        value_part = lax.dynamic_slice_in_dim(value_rows, row_begin, block_size, 0)
        allowed_part = lax.dynamic_slice_in_dim(allowed, row_begin, block_size, 1)
        return attend_block(state_now, queries, key_part, value_part, allowed_part)

    return lax.fori_loop(0, key_count // block_size, step_block, state_in)


def keep_state(current):
    return current


def empty_state(row_count, kv_heads, group_size, head_size):
    maxima = jnp.full((kv_heads, group_size, row_count), lowest, jnp.float32)
    totals = jnp.zeros((kv_heads, group_size, row_count), jnp.float32)
    accumulated = jnp.zeros((kv_heads, group_size, row_count, head_size), jnp.float32)
    return (maxima, totals, accumulated)


def finish(state_in):
    maxima, totals, accumulated = state_in
    safe_totals = jnp.where(totals > 0.0, totals, 1.0)
    result = accumulated / safe_totals[..., None]
    kv_heads, group_size, row_count, head_size = result.shape
    return jnp.transpose(result, (2, 0, 1, 3)).reshape(row_count, kv_heads * group_size * head_size)


def causal_group(current, group, key_rows, value_rows, key_index, offset):
    queries, row_index = group
    allowed = key_index[None, :] <= row_index[:, None]

    def causal_compute(state_in):
        return attend(state_in, queries, key_rows, value_rows, allowed)

    return lax.cond(offset <= jnp.max(row_index), causal_compute, keep_state, current)


def frame_mask(frame_index, lower_frame, upper_frame):
    return jnp.logical_and(
        frame_index[None, :] >= lower_frame[:, None], frame_index[None, :] < upper_frame[:, None]
    )


def on_device(
    query_self,
    key_self,
    value_self,
    positions,
    query_cross,
    key_vision,
    value_vision,
    media_range,
    gate_scale,
):
    head_size = HD
    kv_heads = key_self.shape[1] // head_size
    group_size = query_self.shape[1] // key_self.shape[1]
    row_count = query_self.shape[0]
    vision_count = key_vision.shape[0]
    device = lax.axis_index("ctx")
    own_rows = device * row_count + jnp.arange(row_count, dtype=jnp.int32)
    rotated_query = rotate(
        query_self.astype(jnp.float32).reshape(row_count, kv_heads * group_size, head_size),
        positions,
    )
    rotated_query = rotated_query.astype(jnp.bfloat16).reshape(
        row_count, kv_heads, group_size, head_size
    )
    rotated_key = rotate(
        key_self.astype(jnp.float32).reshape(row_count, kv_heads, head_size), positions
    ).astype(jnp.bfloat16)
    self_values = value_self.reshape(row_count, kv_heads, head_size)
    vision_keys = key_vision.reshape(vision_count, kv_heads, head_size)
    vision_values = value_vision.reshape(vision_count, kv_heads, head_size)
    cross_queries = query_cross.reshape(row_count, kv_heads, group_size, head_size)
    lower_frame = jnp.repeat(media_range[:, 0], TBLOCK)
    upper_frame = jnp.repeat(media_range[:, 1], TBLOCK)
    has_frames = upper_frame > lower_frame
    query_groups = ((rotated_query, own_rows),)
    self_start = tuple(
        (empty_state(group[1].shape[0], kv_heads, group_size, head_size) for group in query_groups)
    )
    cross_start = empty_state(row_count, kv_heads, group_size, head_size)
    offset = jnp.int32(0)
    key_rows = lax.all_gather(rotated_key, "ctx", axis=0, tiled=True)
    value_rows = lax.all_gather(self_values, "ctx", axis=0, tiled=True)
    key_index = jnp.arange(key_rows.shape[0], dtype=jnp.int32)
    updated = []
    for current, group in zip(self_start, query_groups):
        updated.append(causal_group(current, group, key_rows, value_rows, key_index, offset))
    self_states = tuple(updated)
    key_rows = lax.all_gather(vision_keys, "ctx", axis=0, tiled=True)
    value_rows = lax.all_gather(vision_values, "ctx", axis=0, tiled=True)
    frame_index = jnp.arange(key_rows.shape[0], dtype=jnp.int32) // FRAME_LEN
    allowed = frame_mask(frame_index, lower_frame, upper_frame)
    touching = jnp.logical_and(lower_frame <= frame_index[-1], upper_frame > frame_index[0])
    needed = jnp.any(jnp.logical_and(has_frames, touching))

    def fold_compute(state_in):
        return attend(state_in, cross_queries, key_rows, value_rows, allowed)

    cross_state = lax.cond(needed, fold_compute, keep_state, cross_start)
    self_rows = finish(self_states[0]).astype(jnp.bfloat16)
    cross_rows = jnp.where(
        has_frames[:, None], jnp.tanh(gate_scale[0]) * finish(cross_state), 0.0
    ).astype(jnp.bfloat16)
    self_context, cross_context = (
        lax.all_to_all(self_rows, "head", split_axis=0, concat_axis=1, tiled=True),
        lax.all_to_all(cross_rows, "head", split_axis=0, concat_axis=1, tiled=True),
    )
    return (self_context, cross_context)


def solution(mesh):
    placed = (
        P("ctx", "head"),
        P("ctx", "head"),
        P("ctx", "head"),
        P("ctx"),
        P("ctx", "head"),
        P("ctx", "head"),
        P("ctx", "head"),
        P("ctx", None),
        P(),
    )
    return jax.shard_map(
        on_device,
        mesh=mesh,
        in_specs=placed,
        out_specs=(P(("ctx", "head"), None), P(("ctx", "head"), None)),
        check_vma=False,
    )
```

profile of v0, /device:TPU:1, one launch (start us, length us, event | category | flops | bytes accessed | tf_op | source)
XLA Modules:
  0.0 1147.8 jit_solution(11105071938108322923)
XLA Ops:
  14.5 2.0 and_and_fusion
  19.2 250.3 %all-gather.12.cloned.1.call-done = bf16[7168,128]{1,0:T(8,128)(2,1)} async-done(((bf16[56,128]{1,0:T(8,128)(2,1)}), bf16[7168,128]{1,0:T(8,128)(2,1)}) %all-gather.12.cloned.1.call-update) | async-done | bytes 1835024 | tf_op jit(solution)/shard_map/all_gather | solution.py:159
  269.5 263.4 %all-gather.14.cloned.1.call-done = bf16[7168,128]{1,0:T(8,128)(2,1)} async-done(((bf16[56,128]{1,0:T(8,128)(2,1)}), bf16[7168,128]{1,0:T(8,128)(2,1)}) %all-gather.14.cloned.1.call-update) | async-done | bytes 1835024 | tf_op jit(solution)/shard_map/all_gather | solution.py:160
  536.9 24.5 %all-to-all-start.1 = ((bf16[8,8,1024]{2,1,0:T(8,128)(2,1)}), bf16[8,8,1024]{2,1,0:T(8,128)(2,1)S(1)}, u32[]{:S(2)}, u32[]{:S(2)}) async-start(bf16[8,8,1024]{2,1,0:T(8,128)(2,1)} %select_convert_fusion), calls=%async_computation.1 | async-start | bytes 262144 | tf_op jit(solution)/shard_map/all_to_all | solution.py:176
  561.5 235.4 %all-gather.8.cloned.1.call-done = bf16[8192,1,128]{2,0,1:T(8,128)(2,1)} async-done(((bf16[64,1,128]{2,0,1:T(8,128)(2,1)}), bf16[8192,1,128]{2,0,1:T(8,128)(2,1)}) %all-gather.8.cloned.1.call-update) | async-done | bytes 2097168 | tf_op jit(solution)/shard_map/all_gather | solution.py:152
  796.9 263.3 %all-gather.10.cloned.1.call-done = bf16[8192,128]{1,0:T(8,128)(2,1)} async-done(((bf16[64,128]{1,0:T(8,128)(2,1)}), bf16[8192,128]{1,0:T(8,128)(2,1)}) %all-gather.10.cloned.1.call-update) | async-done | bytes 2097168 | tf_op jit(solution)/shard_map/all_gather | solution.py:153
  1060.3 47.1 %conditional.2 = (f32[1,8,64]{2,1,0:T(8,128)}, f32[1,8,64,128]{3,2,1,0:T(8,128)}) conditional(s32[]{:T(128)} %convert_element_type.57, () %tuple.56, (s32[]{:T(128)}, s32[64,1]{0,1:T(1,128)S(1)}, s32[64,8192]{1,0:T(8,128)S(1)}, bf16[8192,1,128]{2,0,1:T(8,128)(2,1)}, bf16[64,1,8,128]{3,2,0,1:T(8,128)(2,1)S(1)}, ...), branch_computations={%region_1.0_spmd, %region_2.7_spmd} | conditional | flops 275975232 | bytes 10716215 | solution.py:102
  1060.8 46.7 %while.37 = (s32[]{:T(128)}, f32[1,8,64]{2,1,0:T(8,128)S(1)}, f32[1,8,64]{2,1,0:T(8,128)}, f32[1,8,64,128]{3,2,1,0:T(8,128)}, pred[64,8192]{1,0:T(8,128)(4,1)S(1...) while((s32[]{:T(128)}, f32[1,8,64]{2,1,0:T(8,128)S(1)}, ...), condition=%wide.region_6.6_spmd.clone, body=%wide.region_3.5_spmd.clone.sunk | while | flops 275450880 | bytes 7831739 | solution.py:73
  1062.3 2.3 fusion.88
  1067.5 2.4 fusion.88
  1071.9 1.5 fusion.85
  1073.4 2.4 fusion.88
  1077.8 1.5 fusion.85
  1079.3 2.4 fusion.88
  1083.8 1.5 fusion.85
  1085.3 2.4 fusion.88
  1089.7 1.5 fusion.85
  1091.2 2.4 fusion.88
  1095.6 1.5 fusion.85
  1097.1 2.4 fusion.88
  1101.5 1.5 fusion.85
  1103.1 2.4 fusion.88
  1110.1 24.6 %all-to-all-start = ((bf16[8,8,1024]{2,1,0:T(8,128)(2,1)}), bf16[8,8,1024]{2,1,0:T(8,128)(2,1)S(1)}, u32[]{:S(2)}, u32[]{:S(2)}) async-start(bf16[8,8,1024]{2,1,0:T(8,128)(2,1)} %convert_element_type.61), calls=%async_computation | async-start | bytes 262144 | tf_op jit(solution)/shard_map/all_to_all | solution.py:175
  1134.7 5.2 all-to-all-done
  (94 shorter events, 35.9 us)
Async XLA Ops:
  7.2 12.0 %copy-start.1 = (s32[4,2]{0,1:T(2,128)S(1)}, s32[4,2]{0,1:T(2,128)}, u32[]{:S(2)}) copy-start(s32[4,2]{0,1:T(2,128)} %param.24) | copy-start | bytes 100
  7.2 525.7 %copy-start = (bf16[64,1024]{1,0:T(8,128)(2,1)S(1)}, bf16[64,1024]{1,0:T(8,128)(2,1)}, u32[]{:S(2)}) copy-start(bf16[64,1024]{1,0:T(8,128)(2,1)} %param.21) | copy-start | bytes 393220
  7.2 262.3 %all-gather.12.cloned.1.call-start = ((), (), s32[]{:S(2)}) async-start(), calls=%async_computation.4 | async-start | bytes 1849344 | tf_op jit(solution)/shard_map/all_gather | solution.py:159
  7.9 525.0 %all-gather.14.cloned.1.call-start = ((), (), s32[]{:S(2)}) async-start(), calls=%async_computation.5 | async-start | bytes 1849344 | tf_op jit(solution)/shard_map/all_gather | solution.py:160
  8.7 788.2 %all-gather.8.cloned.1.call-start = ((), (), s32[]{:S(2)}) async-start(), calls=%async_computation.2 | async-start | bytes 2113536 | tf_op jit(solution)/shard_map/all_gather | solution.py:152
  11.0 1049.2 %all-gather.10.cloned.1.call-start = ((), (), s32[]{:S(2)}) async-start(), calls=%async_computation.3 | async-start | bytes 2113536 | tf_op jit(solution)/shard_map/all_gather | solution.py:153
  536.9 573.1 %all-to-all-start.1 = ((bf16[8,8,1024]{2,1,0:T(8,128)(2,1)}), bf16[8,8,1024]{2,1,0:T(8,128)(2,1)S(1)}, u32[]{:S(2)}, u32[]{:S(2)}) async-start(bf16[8,8,1024]{2,1,0:T(8,128)(2,1)} %select_convert_fusion), calls=%async_computation.1 | async-start | bytes 262144 | tf_op jit(solution)/shard_map/all_to_all | solution.py:176
  1110.1 29.9 %all-to-all-start = ((bf16[8,8,1024]{2,1,0:T(8,128)(2,1)}), bf16[8,8,1024]{2,1,0:T(8,128)(2,1)S(1)}, u32[]{:S(2)}, u32[]{:S(2)}) async-start(bf16[8,8,1024]{2,1,0:T(8,128)(2,1)} %convert_element_type.61), calls=%async_computation | async-start | bytes 262144 | tf_op jit(solution)/shard_map/all_to_all | solution.py:175
Sparse Core Ops, SparseCore 0:
  12.1 257.2 all-gather.11
  273.6 259.2 all-gather.13
  537.6 259.2 all-gather.7
  800.8 259.2 all-gather.9
where the time goes:
time: 1150 us
  waiting for transfers between devices  1020 us (89%)
  starting transfers between devices  49.3 us (4%)
  matrix products  31.2 us (3%)
  other arithmetic  26.8 us (2%)
  between operations  15.9 us (1%)
    all_gather x1, waiting for transfers between devices, on_device(): value_rows = lax.all_gather(vision_values, 'ctx', axis=0, tiled=True)  263 us
    all_gather x1, waiting for transfers between devices, on_device(): value_rows = lax.all_gather(self_values, 'ctx', axis=0, tiled=True)  263 us
    all_gather x1, waiting for transfers between devices, on_device(): key_rows = lax.all_gather(vision_keys, 'ctx', axis=0, tiled=True)  250 us
    all_gather x1, waiting for transfers between devices, on_device(): key_rows = lax.all_gather(rotated_key, 'ctx', axis=0, tiled=True)  235 us
    all_to_all x1, starting transfers between devices, on_device(): lax.all_to_all(self_rows, 'head', split_axis=0, concat_axis=1, tiled=True)  24.6 us
    all_to_all x1, starting transfers between devices, on_device(): lax.all_to_all(cross_rows, 'head', split_axis=0, concat_axis=1, tiled=True)  24.5 us
  transfers between devices with their start and end apart: 6, of which 5 were waited for; matrix products, arithmetic and copies ran while one was open for 5% of the time, Pallas kernels for 0%

commit v1 on v0

v1 whole, which is shorter than its diff:
```python
import functools
import math

import jax
import jax.numpy as jnp
from jax import lax
from jax.experimental import pallas as pl
from jax.experimental.pallas import tpu as pltpu
from jax.sharding import PartitionSpec as P

HD = 128
TBLOCK = 16
FRAME_LEN = 896
NY = 4
ROPE_BASE = 500000.0
BIG = 1e30
LOWEST = -3e38
LOG2 = HD ** -0.5 * math.log2(math.e)
MESH = pl.DeviceIdType.MESH
F32 = jnp.float32
BF16 = jnp.bfloat16


def prepare_kernel(qs, ks, vs, qc, kf, vf, cos, sin, qa, o_qs, o_qc, o_kv):
    rows = qs.shape[0]
    heads = qs.shape[1] // HD
    cosine = cos[...]
    sine = sin[...]

    def turned(x):
        x = x.astype(F32)
        return (x * cosine + pltpu.roll(x, HD // 2, 1) * sine).astype(BF16)

    o_kv[0:rows, 0:HD] = turned(ks[...])
    o_kv[0:rows, HD:] = vs[...]
    pad = jnp.zeros((rows - kf.shape[0], HD), F32)
    o_kv[rows:, 0:HD] = jnp.concatenate([kf[...].astype(F32), pad], 0).astype(BF16)
    o_kv[rows:, HD:] = jnp.concatenate([vf[...].astype(F32), pad], 0).astype(BF16)
    for h in range(heads):
        cut = slice(h * HD, (h + 1) * HD)
        o_qs[:, cut] = turned(qs[:, cut])
    o_qc[:, 0 : heads * HD] = qc[...]
    o_qc[:, heads * HD :] = qa[...]


def main_kernel(
    nz, ny, nh, real, zpf,
    qs, qc, kv, gate, out_s, out_c,
    kvb, qsb, qcb, qat, m_s, l_s, acc_s, m_c, l_c, acc_c,
    osb, ocb, stb, rsb, rcb, rst, fsb, fcb,
    r_ring, s_ring, r_q, s_q, r_o, s_o, r_f, s_f, loc,
):
    rows = qs.shape[0]
    heads = qs.shape[1] // HD
    toks = ny * rows
    half = nz // 2
    groups = nz // 4
    ctx = lax.axis_index("ctx")
    head = lax.axis_index("head")
    z = ctx // ny
    y = ctx % ny
    z_up = (z + 1) % nz
    z_dn = (z + nz - 1) % nz

    def at_z(other):
        return (other * ny + y, head)

    def at_y(other):
        return (z * ny + other, head)

    def at_h(other):
        return (ctx, other)

    def slot(offset):
        return (z + nz + offset) % nz

    def ring(flow, d, piece):
        src_slot = slot(d - 1) if flow == 0 else slot(1 - d)
        part = pl.ds(piece * rows, rows)
        return pltpu.make_async_remote_copy(
            src_ref=kvb.at[src_slot, part, :],
            dst_ref=kvb.at[src_slot, part, :],
            send_sem=s_ring.at[flow, d, piece],
            recv_sem=r_ring.at[flow, d, piece],
            device_id=at_z(z_dn if flow == 0 else z_up),
            device_id_type=MESH,
        )

    def ring_in(flow, d, piece):
        dst_slot = slot(d) if flow == 0 else slot(-d)
        part = pl.ds(piece * rows, rows)
        return pltpu.make_async_remote_copy(
            src_ref=kvb.at[dst_slot, part, :],
            dst_ref=kvb.at[dst_slot, part, :],
            send_sem=s_ring.at[flow, d, piece],
            recv_sem=r_ring.at[flow, d, piece],
            device_id=at_z(z_dn if flow == 0 else z_up),
            device_id_type=MESH,
        )

    def q_copy(kind, i):
        src, dst = ((qs, qsb), (qc, qcb))[kind]
        return pltpu.make_async_remote_copy(
            src_ref=src,
            dst_ref=dst.at[y],
            send_sem=s_q.at[kind, i],
            recv_sem=r_q.at[kind, i],
            device_id=at_y((y + i) % ny),
            device_id_type=MESH,
        )

    def q_in(kind, i):
        src, dst = ((qs, qsb), (qc, qcb))[kind]
        return pltpu.make_async_remote_copy(
            src_ref=src,
            dst_ref=dst.at[(y + ny - i) % ny],
            send_sem=s_q.at[kind, i],
            recv_sem=r_q.at[kind, i],
            device_id=at_y((y + i) % ny),
            device_id_type=MESH,
        )

    def o_copy(kind, i):
        src, dst = ((osb, rsb), (ocb, rcb), (stb, rst))[kind]
        return pltpu.make_async_remote_copy(
            src_ref=src.at[(y + i) % ny],
            dst_ref=dst.at[i],
            send_sem=s_o.at[kind, i],
            recv_sem=r_o.at[kind, i],
            device_id=at_y((y + i) % ny),
            device_id_type=MESH,
        )

    wide = heads * HD

    def f_copy(kind, i):
        src, dst = ((fsb, out_s), (fcb, out_c))[kind]
        other = (head + i) % nh
        return pltpu.make_async_remote_copy(
            src_ref=src.at[other],
            dst_ref=dst.at[:, pl.ds(pl.multiple_of(head * wide, wide), wide)],
            send_sem=s_f.at[kind, i],
            recv_sem=r_f.at[kind, i],
            device_id=at_h(other),
            device_id_type=MESH,
        )

    def f_in(kind, i):
        src, dst = ((fsb, out_s), (fcb, out_c))[kind]
        other = (head + nh - i) % nh
        return pltpu.make_async_remote_copy(
            src_ref=src.at[other],
            dst_ref=dst.at[:, pl.ds(pl.multiple_of(other * wide, wide), wide)],
            send_sem=s_f.at[kind, i],
            recv_sem=r_f.at[kind, i],
            device_id=at_h((head + i) % nh),
            device_id_type=MESH,
        )

    own_kv = pltpu.make_async_copy(kv, kvb.at[z], loc.at[0])
    own_qs = pltpu.make_async_copy(qs, qsb.at[y], loc.at[1])
    own_qc = pltpu.make_async_copy(qc, qcb.at[y], loc.at[2])
    own_kv.start()
    own_qs.start()
    own_qc.start()

    barrier = pltpu.get_barrier_semaphore()
    partners = [at_z(z_up), at_z(z_dn)]
    partners += [at_y((y + i) % ny) for i in range(1, ny)]
    partners += [at_h((head + i) % nh) for i in range(1, nh)]
    for partner in partners:
        pl.semaphore_signal(barrier, inc=1, device_id=partner, device_id_type=MESH)
    pl.semaphore_wait(barrier, len(partners))

    own_kv.wait()
    for piece in range(2):
        ring(0, 1, piece).start()
        ring(1, 1, piece).start()
    for kind in range(2):
        for i in range(1, ny):
            q_copy(kind, i).start()

    lane = lax.broadcasted_iota(jnp.int32, (toks, HD), 1)
    token = lax.broadcasted_iota(jnp.int32, (toks, HD), 0)
    late = jnp.logical_and(lane < nz, lane > z)
    ahead = jnp.logical_and(lane >= rows, y * rows + lane - rows > token)
    qat[...] = jnp.where(jnp.logical_or(late, ahead), -BIG, 0.0).astype(BF16)

    @pl.loop(0, heads)
    def _(h):
        m_s[h] = jnp.full((toks, HD), LOWEST, F32)
        m_c[h] = jnp.full((toks, HD), LOWEST, F32)
        l_s[h] = jnp.zeros((toks, HD), F32)
        l_c[h] = jnp.zeros((toks, HD), F32)
        acc_s[h] = jnp.zeros((toks, HD), F32)
        acc_c[h] = jnp.zeros((toks, HD), F32)

    own_qs.wait()
    own_qc.wait()

    def serve(d, piece):
        ring_in(0, d, piece).wait_recv()

        @pl.when(d < half)
        def _():
            ring(0, d + 1, piece).start()

        @pl.when(d < half)
        def _():
            ring_in(1, d, piece).wait_recv()

        @pl.when(d < half - 1)
        def _():
            ring(1, d + 1, piece).start()

    def keys_of(kind, group):
        offsets = (-2 * group, -2 * group - 1, 2 * group + 1, 2 * group + 2)
        keys, marks, values = [], [], []
        lanes = lax.broadcasted_iota(jnp.int32, (rows, HD), 1)
        index = lax.broadcasted_iota(jnp.int32, (rows, HD), 0)
        for offset in offsets:
            at = slot(offset)
            part = slice(kind * rows, (kind + 1) * rows)
            keys.append(kvb[at, part, 0:HD])
            values.append(kvb[at, part, HD:])
            if kind == 0:
                mark = jnp.where(at == z, rows + index, at)
            else:
                mark = jnp.where(index < real, at // zpf, HD - 1)
            marks.append(jnp.where(lanes == mark, 1.0, 0.0).astype(BF16))
        key = jnp.concatenate([jnp.concatenate(keys, 0), jnp.concatenate(marks, 0)], 1)
        return key, jnp.concatenate(values, 0)

    def attend(kind, group, head_list):
        key, value = keys_of(kind, group)
        qb = (qsb, qcb)[kind]
        m_r, l_r, acc_r = ((m_s, l_s, acc_s), (m_c, l_c, acc_c))[kind]
        if kind == 0:
            extra = qat[...]
        else:
            extra = qcb[:, :, wide:].reshape(toks, HD)
        for h in head_list:
            q = qb[:, :, h * HD : (h + 1) * HD].reshape(toks, HD)
            scores = lax.dot_general(
                jnp.concatenate([q, extra], 1), key,
                (((1,), (1,)), ((), ())), preferred_element_type=F32,
            )
            m_old = m_r[h]
            m_new = jnp.maximum(m_old, jnp.max(scores, axis=1, keepdims=True))
            m_r[h] = m_new
            alpha = jnp.exp2((m_old - m_new) * LOG2)
            weights = jnp.exp2((scores - m_new[:, 0:1]) * LOG2)
            total = weights[:, 0:HD]
            for b in range(1, weights.shape[1] // HD):
                total = total + weights[:, b * HD : (b + 1) * HD]
            l_r[h] = l_r[h] * alpha + total
            acc_r[h] = acc_r[h] * alpha + jnp.dot(
                weights.astype(BF16), value, preferred_element_type=F32
            )

    low = tuple(range(heads // 2))
    high = tuple(range(heads // 2, heads))

    @pl.loop(0, groups + 1)
    def _(g):
        for turn in range(4):
            @pl.when(g < groups)
            def _():
                serve(2 * g + 1 + turn // 2, turn % 2)

            if turn % 2 == 0:
                @pl.when(g == 1)
                def _():
                    for i in range(1, ny):
                        q_in(turn // 2, i).wait_recv()

            @pl.when(g > 0)
            def _():
                attend(turn // 2, g - 1, (low, high)[turn % 2])

    lane = lax.broadcasted_iota(jnp.int32, (toks, HD), 1)
    stats = jnp.zeros((toks, HD), F32)
    for kind in range(2):
        m_r, l_r, acc_r = ((m_s, l_s, acc_s), (m_c, l_c, acc_c))[kind]
        dst = (osb, ocb)[kind]
        for h in range(heads):
            total = jnp.sum(l_r[h], axis=1, keepdims=True)
            part = acc_r[h] / total
            dst[:, :, h * HD : (h + 1) * HD] = part.astype(BF16).reshape(ny, rows, HD)
            level = m_r[h] * LOG2 + jnp.log2(total)
            stats = jnp.where(lane == kind * heads + h, level, stats)
        if kind == 1:
            stb[...] = stats.reshape(ny, rows, HD)
        for i in range(1, ny):
            o_copy(kind, i).start()
    for i in range(1, ny):
        o_copy(2, i).start()

    for i in range(1, ny):
        o_copy(2, i).wait_recv()
    levels = [stb[y]] + [rst[i] for i in range(1, ny)]
    top = levels[0]
    for level in levels[1:]:
        top = jnp.maximum(top, level)
    shares = [jnp.exp2(level - top) for level in levels]
    whole = shares[0]
    for share in shares[1:]:
        whole = whole + share
    shares = [share / whole for share in shares]
    for kind in range(2):
        mine, other = ((osb, rsb), (ocb, rcb))[kind]
        final, out = ((fsb, out_s), (fcb, out_c))[kind]
        for i in range(1, ny):
            o_copy(kind, i).wait_recv()
        for h in range(heads):
            cut = slice(h * HD, (h + 1) * HD)
            at = kind * heads + h
            mixed = mine[y, :, cut].astype(F32) * shares[0][:, at : at + 1]
            for i in range(1, ny):
                mixed = mixed + other[i, :, cut].astype(F32) * shares[i][:, at : at + 1]
            if kind == 1:
                mixed = mixed * gate[...]
            final[:, :, cut] = mixed.reshape(nh, rows // nh, HD).astype(BF16)
        for i in range(1, nh):
            f_copy(kind, i).start()
        pltpu.make_async_copy(
            final.at[head],
            out.at[:, pl.ds(pl.multiple_of(head * wide, wide), wide)],
            loc.at[3 + kind],
        ).start()
    for kind in range(2):
        final, out = ((fsb, out_s), (fcb, out_c))[kind]
        for i in range(1, nh):
            f_in(kind, i).wait_recv()
        pltpu.make_async_copy(
            final.at[head],
            out.at[:, pl.ds(pl.multiple_of(head * wide, wide), wide)],
            loc.at[3 + kind],
        ).wait()

    @pl.loop(1, half)
    def _(d):
        for flow in range(2):
            for piece in range(2):
                ring(flow, d, piece).wait_send()

    for piece in range(2):
        ring(0, half, piece).wait_send()
    for kind in range(2):
        for i in range(1, ny):
            q_copy(kind, i).wait_send()
    for kind in range(3):
        for i in range(1, ny):
            o_copy(kind, i).wait_send()
    for kind in range(2):
        for i in range(1, nh):
            f_copy(kind, i).wait_send()


def on_device(
    nctx, nh,
    query_self, key_self, value_self, positions,
    query_cross, key_vision, value_vision, media_range, gate_scale,
):
    rows, wide = query_self.shape
    real = key_vision.shape[0]
    ny = NY
    nz = nctx // ny
    heads = wide // HD
    toks = ny * rows
    zpf = FRAME_LEN // (real * ny)

    exponents = jnp.arange(HD // 2, dtype=F32) * (2.0 / HD)
    frequency = jnp.power(ROPE_BASE, -exponents)
    angles = positions.astype(F32)[:, None] * jnp.tile(frequency, 2)[None, :]
    first = jnp.arange(HD)[None, :] < HD // 2
    cosine = jnp.cos(angles)
    sine = jnp.where(first, -jnp.sin(angles), jnp.sin(angles))

    lower = jnp.repeat(media_range[:, 0], TBLOCK)[:, None]
    upper = jnp.repeat(media_range[:, 1], TBLOCK)[:, None]
    lanes = jnp.arange(HD, dtype=jnp.int32)[None, :]
    hidden = jnp.logical_or(lanes < lower, lanes >= upper)
    hidden = jnp.logical_and(hidden, lanes < nz // zpf)
    hidden = jnp.logical_or(hidden, lanes == HD - 1)
    extra = jnp.where(hidden, -BIG, 0.0).astype(BF16)
    gate = jnp.where(upper > lower, jnp.tanh(gate_scale[0]), 0.0)
    gate = jnp.broadcast_to(gate, (rows, HD)).astype(F32)

    vmem = pl.BlockSpec(memory_space=pltpu.VMEM)
    qs, qc, kv = pl.pallas_call(
        prepare_kernel,
        out_shape=(
            jax.ShapeDtypeStruct((rows, wide), BF16),
            jax.ShapeDtypeStruct((rows, wide + HD), BF16),
            jax.ShapeDtypeStruct((2 * rows, 2 * HD), BF16),
        ),
        in_specs=[vmem] * 9,
        out_specs=(vmem,) * 3,
        name="prepare",
    )(query_self, key_self, value_self, query_cross, key_vision, value_vision, cosine, sine, extra)

    state = pltpu.VMEM((heads, toks, HD), F32)
    part = pltpu.VMEM((ny, rows, wide), BF16)
    stat = pltpu.VMEM((ny, rows, HD), F32)
    final = pltpu.VMEM((nh, rows // nh, wide), BF16)
    dma = pltpu.SemaphoreType.DMA
    half = nz // 2
    return pl.pallas_call(
        functools.partial(main_kernel, nz, ny, nh, real, zpf),
        out_shape=(jax.ShapeDtypeStruct((rows // nh, wide * nh), BF16),) * 2,
        in_specs=[vmem] * 4,
        out_specs=(vmem,) * 2,
        scratch_shapes=[
            pltpu.VMEM((nz, 2 * rows, 2 * HD), BF16),
            part,
            pltpu.VMEM((ny, rows, wide + HD), BF16),
            pltpu.VMEM((toks, HD), BF16),
            state, state, state, state, state, state,
            part, part, stat, part, part, stat, final, final,
            dma((2, half + 1, 2)), dma((2, half + 1, 2)),
            dma((2, ny)), dma((2, ny)),
            dma((3, ny)), dma((3, ny)),
            dma((2, nh)), dma((2, nh)),
            dma((5,)),
        ],
        compiler_params=pltpu.CompilerParams(
            collective_id=0, has_side_effects=True, vmem_limit_bytes=40 * 1024 * 1024
        ),
        name="attend",
    )(qs, qc, kv, gate)


def solution(mesh):
    placed = (
        P("ctx", "head"),
        P("ctx", "head"),
        P("ctx", "head"),
        P("ctx"),
        P("ctx", "head"),
        P("ctx", "head"),
        P("ctx", "head"),
        P("ctx", None),
        P(),
    )
    body = functools.partial(on_device, mesh.shape["ctx"], mesh.shape["head"])
    return jax.shard_map(
        body,
        mesh=mesh,
        in_specs=placed,
        out_specs=(P(("ctx", "head"), None), P(("ctx", "head"), None)),
        check_vma=False,
    )
```

time: 1150 us -> 113 us (0.10)
  waiting for transfers between devices: 1020 us -> 0 us
  Pallas kernels: 0 us -> 104 us
  starting transfers between devices: 49.3 us -> 0 us
  matrix products: 31.2 us -> 0 us
  other arithmetic: 26.8 us -> 1.57 us
  between operations: 15.9 us -> 1.35 us
    all_gather x4 -> x0, waiting for transfers between devices: 1010 us -> none  [the longest x1 263 us: on_device(): value_rows = lax.all_gather(vision_values, 'ctx', axis=0, tiled=True)]
    pallas_call x0 -> x2, Pallas kernels: none -> 104 us  [the longest x1 102 us: on_device(): pl.pallas_call(functools.partial(main_kernel, nz, ny, nh, real, zpf), out...]
    all_to_all x2 -> x0, starting transfers between devices: 49.2 us -> none  [the longest x1 24.6 us: on_device(): lax.all_to_all(self_rows, 'head', split_axis=0, concat_axis=1, tiled=True)]
    dot_general x16 -> x0, matrix products: 31.2 us -> none  [the longest x8 19.2 us: attend_block(): jnp.einsum('kgrn,nkd->kgrd', weights.astype(jnp.bfloat16), value_rows, pr...]
  transfers between devices with their start and end apart: 6 -> 0, of which waited for: 5 -> 0; matrix products, arithmetic and copies ran while one was open for 5% -> 0% of each run, Pallas kernels for 0% -> 0%
where the time goes in v1:
time: 113 us
  Pallas kernels  104 us (92%)
  local copies, waits for them, and re-layouts  5.76 us (5%)
  other arithmetic  1.57 us (1%)
  between operations  1.35 us (1%)
    pallas_call x1, Pallas kernels, on_device(): pl.pallas_call(functools.partial(main_kernel, nz, ny, nh, real, zpf), out...  102 us
    unnamed x12, local copies, waits for them, and re-layouts  5.29 us

profile of v1, /device:TPU:1, one launch (start us, length us, event | category | flops | bytes accessed | tf_op | source)
XLA Modules:
  0.0 112.6 jit_solution(2174764796463207188)
XLA Ops:
  1.3 0.0 copy-start.4
  1.3 0.6 copy-done.4
  2.0 0.1 mul.28
  2.1 0.0 copy-start.3
  2.1 0.7 copy-done.3
  2.8 0.1 broadcast_in_dim.39
  2.8 0.1 lt.42
  2.9 0.1 broadcast_in_dim.40
  3.0 0.1 ge.6
  3.1 0.7 select_convert_fusion.qa
  3.8 0.1 broadcast_in_dim.45.gate
  3.8 0.9 negate_select_fusion
  4.7 1.8 %prepare.1 = (bf16[64,1024]{1,0:T(8,128)(2,1)}, bf16[64,1152]{1,0:T(8,128)(2,1)}, bf16[128,256]{1,0:T(8,128)(2,1)}) custom-call(bf16[64,1024]{1,0:T(8,128)(2,1)} %qs.1, bf16[64,128]{1,0:T(8,128)(2,1)} %ks.1, bf16[64,128]{1,0:T(8,128)(2,1)} %vs.1, bf16[64,1024]{1,0:T(8,128)(2,1)} %qc.1, bf16[56,128]{1,0:T(8,128)(2,1)} %kf.1, bf16[56,128]{1,0:T(8,128)(2,1)} %vf.1, ...), custom_call_target="tpu_custom_call" | custom-call | tf_op jit(solution)/shard_map/prepare/pallas_call | solution.py:391
  6.5 0.0 copy-start
  6.5 0.9 copy-done
  7.4 0.0 copy-start.1
  7.4 0.9 copy-done.1
  8.3 0.0 copy-start.2
  8.3 0.8 copy-done.2
  9.1 102.1 %attend.1 = (bf16[8,8192]{1,0:T(8,128)(2,1)S(1)}, bf16[8,8192]{1,0:T(8,128)(2,1)S(1)}) custom-call(bf16[64,1024]{1,0:T(8,128)(2,1)S(1)} %copy-done.1, bf16[64,1152]{1,0:T(8,128)(2,1)S(1)} %copy-done, bf16[128,256]{1,0:T(8,128)(2,1)S(1)} %copy-done.2, f32[64,128]{1,0:T(8,128)S(1)} %broadcast_in_dim.45.gate), custom_call_target="tpu_custom_call" | custom-call | tf_op jit(solution)/shard_map/attend/pallas_call | solution.py:409
  111.3 0.7 copy.14
  112.0 0.7 copy.15
  (7 shorter events, 0.0 us)
Async XLA Ops:
  1.3 0.7 copy-start.4
  2.1 0.7 copy-start.3
  6.5 0.9 copy-start
  7.4 0.9 copy-start.1
  8.3 0.8 copy-start.2

commit v2 on v1

v2 whole, which is shorter than its diff:
```python
import functools
import math

import jax
import jax.numpy as jnp
from jax import lax
from jax.experimental import pallas as pl
from jax.experimental.pallas import tpu as pltpu
from jax.sharding import PartitionSpec as P

HD = 128
TBLOCK = 16
FRAME_LEN = 896
NY = 4
ROPE_BASE = 500000.0
BIG = 1e30
LOWEST = -3e38
LOG2 = HD ** -0.5 * math.log2(math.e)
MESH = pl.DeviceIdType.MESH
F32 = jnp.float32
BF16 = jnp.bfloat16


def prepare_kernel(qs, ks, vs, qc, kf, vf, cos, sin, qa, o_qs, o_qc, o_kv):
    rows = qs.shape[0]
    heads = qs.shape[1] // HD
    cosine = cos[...]
    sine = sin[...]

    def turned(x):
        x = x.astype(F32)
        return (x * cosine + pltpu.roll(x, HD // 2, 1) * sine).astype(BF16)

    o_kv[0:rows, 0:HD] = turned(ks[...])
    o_kv[0:rows, HD:] = vs[...]
    pad = jnp.zeros((rows - kf.shape[0], HD), F32)
    o_kv[rows:, 0:HD] = jnp.concatenate([kf[...].astype(F32), pad], 0).astype(BF16)
    o_kv[rows:, HD:] = jnp.concatenate([vf[...].astype(F32), pad], 0).astype(BF16)
    for h in range(heads):
        cut = slice(h * HD, (h + 1) * HD)
        o_qs[:, cut] = turned(qs[:, cut])
    o_qc[:, 0 : heads * HD] = qc[...]
    o_qc[:, heads * HD :] = qa[...]


def main_kernel(
    nz, ny, nh, real, zpf,
    qs, qc, kv, gate, out_s, out_c,
    kvb, qsb, qcb, qat, m_s, l_s, acc_s, m_c, l_c, acc_c,
    scb, rel, osb, ocb, stb, rsb, rcb, rst, fsb, fcb,
    r_ring, s_ring, r_q, s_q, r_o, s_o, r_r, s_r, r_f, s_f, loc,
):
    rows = qs.shape[0]
    wide = qs.shape[1]
    heads = wide // HD
    packed = heads // 2
    span = packed * rows
    half = nz // 2
    groups = nz // 4
    ctx = lax.axis_index("ctx")
    head = lax.axis_index("head")
    z = ctx // ny
    y = ctx % ny
    z_up = (z + 1) % nz
    z_dn = (z + nz - 1) % nz

    def at_z(other):
        return (other * ny + y, head)

    def at_y(i):
        return (z * ny + (y + i) % ny, head)

    def at_h(i):
        return (ctx, (head + i) % nh)

    def slot(offset):
        return (z + nz + offset) % nz

    def ring(flow, d, piece, first=False):
        at = slot(d - 1) if flow == 0 else slot(1 - d)
        part = pl.ds(piece * rows, rows)
        return pltpu.make_async_remote_copy(
            src_ref=kv.at[part, :] if first else kvb.at[at, part, :],
            dst_ref=kvb.at[at, part, :],
            send_sem=s_ring.at[flow, d, piece],
            recv_sem=r_ring.at[flow, d, piece],
            device_id=at_z(z_dn if flow == 0 else z_up),
            device_id_type=MESH,
        )

    def ring_in(flow, d, piece):
        at = slot(d) if flow == 0 else slot(-d)
        part = pl.ds(piece * rows, rows)
        return pltpu.make_async_remote_copy(
            src_ref=kvb.at[at, part, :],
            dst_ref=kvb.at[at, part, :],
            send_sem=s_ring.at[flow, d, piece],
            recv_sem=r_ring.at[flow, d, piece],
            device_id=at_z(z_dn if flow == 0 else z_up),
            device_id_type=MESH,
        )

    def q_copy(kind, i):
        src, dst = ((qs, qsb), (qc, qcb))[kind]
        return pltpu.make_async_remote_copy(
            src_ref=src,
            dst_ref=dst.at[ny - i],
            send_sem=s_q.at[kind, ny - i],
            recv_sem=r_q.at[kind, ny - i],
            device_id=at_y(i),
            device_id_type=MESH,
        )

    def q_relay(kind):
        dst = (qsb, qcb)[kind]
        came, goes = ((ny - 1, 1), (1, ny - 1))[kind]
        return pltpu.make_async_remote_copy(
            src_ref=dst.at[came],
            dst_ref=dst.at[2],
            send_sem=s_q.at[kind, 2],
            recv_sem=r_q.at[kind, 2],
            device_id=at_y(goes),
            device_id_type=MESH,
        )

    def o_copy(kind, i):
        src, dst = ((osb, rsb), (ocb, rcb))[kind]
        return pltpu.make_async_remote_copy(
            src_ref=src.at[i],
            dst_ref=dst.at[ny - i],
            send_sem=s_o.at[kind, ny - i],
            recv_sem=r_o.at[kind, ny - i],
            device_id=at_y(i),
            device_id_type=MESH,
        )

    def o_half(kind, j):
        src = (osb, ocb)[kind]
        return pltpu.make_async_remote_copy(
            src_ref=src.at[2, :, pl.ds(j * span, span)],
            dst_ref=rel.at[kind, j],
            send_sem=s_r.at[kind, j],
            recv_sem=r_r.at[kind, j],
            device_id=at_y((1, ny - 1)[j]),
            device_id_type=MESH,
        )

    def o_relay(kind, j):
        dst = (rsb, rcb)[kind]
        return pltpu.make_async_remote_copy(
            src_ref=rel.at[kind, j],
            dst_ref=dst.at[2, :, pl.ds(j * span, span)],
            send_sem=s_r.at[kind, 2 + j],
            recv_sem=r_r.at[kind, 2 + j],
            device_id=at_y((1, ny - 1)[j]),
            device_id_type=MESH,
        )

    def t_copy(kind, i):
        return pltpu.make_async_remote_copy(
            src_ref=stb.at[kind, i],
            dst_ref=rst.at[kind, ny - i],
            send_sem=s_o.at[2 + kind, ny - i],
            recv_sem=r_o.at[2 + kind, ny - i],
            device_id=at_y(i),
            device_id_type=MESH,
        )

    def f_copy(kind, i):
        src, dst = ((fsb, out_s), (fcb, out_c))[kind]
        return pltpu.make_async_remote_copy(
            src_ref=src.at[(head + i) % nh],
            dst_ref=dst.at[:, pl.ds(pl.multiple_of(head * wide, wide), wide)],
            send_sem=s_f.at[kind, i],
            recv_sem=r_f.at[kind, i],
            device_id=at_h(i),
            device_id_type=MESH,
        )

    def f_in(kind, i):
        src, dst = ((fsb, out_s), (fcb, out_c))[kind]
        other = (head + nh - i) % nh
        return pltpu.make_async_remote_copy(
            src_ref=src.at[other],
            dst_ref=dst.at[:, pl.ds(pl.multiple_of(other * wide, wide), wide)],
            send_sem=s_f.at[kind, i],
            recv_sem=r_f.at[kind, i],
            device_id=at_h(i),
            device_id_type=MESH,
        )

    own_kv = pltpu.make_async_copy(kv, kvb.at[z], loc.at[0])
    own_qs = pltpu.make_async_copy(qs, qsb.at[0], loc.at[1])
    own_qc = pltpu.make_async_copy(qc, qcb.at[0], loc.at[2])
    own_kv.start()
    own_qs.start()
    own_qc.start()

    barrier = pltpu.get_barrier_semaphore()
    partners = [at_z(z_up), at_z(z_dn)]
    partners += [at_y(i) for i in range(1, ny)]
    partners += [at_h(i) for i in range(1, nh)]
    for partner in partners:
        pl.semaphore_signal(barrier, inc=1, device_id=partner, device_id_type=MESH)
    pl.semaphore_wait(barrier, len(partners))

    for piece in range(2):
        ring(0, 1, piece, True).start()
        ring(1, 1, piece, True).start()
    for kind in range(2):
        for i in (1, ny - 1):
            q_copy(kind, i).start()

    lane = lax.broadcasted_iota(jnp.int32, (rows, HD), 1)
    token = lax.broadcasted_iota(jnp.int32, (rows, HD), 0)
    late = jnp.logical_and(lane < nz, lane > z)
    for i in range(ny):
        place = ((y + i) % ny - y) * rows + token
        ahead = jnp.logical_and(lane >= rows, lane - rows > place)
        qat[i] = jnp.where(jnp.logical_or(late, ahead), -BIG, 0.0).astype(BF16)
    for m_r, l_r in ((m_s, l_s), (m_c, l_c)):
        m_r[...] = jnp.full(m_r.shape, LOWEST, F32)
        l_r[...] = jnp.zeros(l_r.shape, F32)

    @pl.loop(0, 2 * ny)
    def _(b):
        acc_s[b] = jnp.zeros((HD, span), F32)
        acc_c[b] = jnp.zeros((HD, span), F32)

    own_kv.wait()
    own_qs.wait()
    own_qc.wait()

    def serve(d, piece):
        ring_in(0, d, piece).wait_recv()

        @pl.when(d < half)
        def _():
            ring(0, d + 1, piece).start()

        @pl.when(d < half)
        def _():
            ring_in(1, d, piece).wait_recv()

        @pl.when(d < half - 1)
        def _():
            ring(1, d + 1, piece).start()

    def keys_of(kind, group):
        offsets = (-2 * group, -2 * group - 1, 2 * group + 1, 2 * group + 2)
        keys, marks, values = [], [], []
        lanes = lax.broadcasted_iota(jnp.int32, (rows, HD), 1)
        index = lax.broadcasted_iota(jnp.int32, (rows, HD), 0)
        for offset in offsets:
            at = slot(offset)
            part = slice(kind * rows, (kind + 1) * rows)
            keys.append(kvb[at, part, 0:HD])
            values.append(kvb[at, part, HD:])
            if kind == 0:
                mark = jnp.where(at == z, rows + index, at)
            else:
                mark = jnp.where(index < real, at // zpf, HD - 1)
            marks.append(jnp.where(lanes == mark, 1.0, 0.0).astype(BF16))
        key = jnp.concatenate([jnp.concatenate(keys, 0), jnp.concatenate(marks, 0)], 1)
        value = jnp.concatenate(values, 0).astype(F32)
        return key, jnp.transpose(value).astype(BF16)

    def q_wait(kind, i):
        if i == 2:
            q_relay(kind).wait_recv()
        elif i > 0:
            q_copy(kind, ny - i).wait_recv()

    def attend(kind, group, sources):
        key, value = keys_of(kind, group)
        qb = (qsb, qcb)[kind]
        m_r, l_r, acc_r = ((m_s, l_s, acc_s), (m_c, l_c, acc_c))[kind]

        def score(i, j, turn):
            b = 2 * i + j
            extra = qat[i] if kind == 0 else qcb[i, :, wide:]
            parts = [
                qb[i, :, h * HD : (h + 1) * HD]
                for h in range(j * packed, (j + 1) * packed)
            ]
            q = jnp.concatenate(
                [jnp.concatenate(parts, 0), jnp.concatenate([extra] * packed, 0)], 1
            )
            scores = lax.dot_general(
                key, q, (((1,), (1,)), ((), ())), preferred_element_type=F32
            )
            scb[turn] = scores
            m_old = m_r[b : b + 1, :]
            m_new = jnp.maximum(m_old, jnp.max(scores, axis=0, keepdims=True))
            m_r[b : b + 1, :] = m_new
            return m_new, jnp.exp2((m_old - m_new) * LOG2)

        def fold(i, j, turn, m_new, alpha):
            b = 2 * i + j
            weights = jnp.exp2((scb[turn] - m_new) * LOG2)
            l_r[b : b + 1, :] = l_r[b : b + 1, :] * alpha + jnp.sum(
                weights, axis=0, keepdims=True
            )
            acc_r[b] = acc_r[b] * alpha + jnp.dot(
                value, weights.astype(BF16), preferred_element_type=F32
            )

        blocks = [(i, j) for i in sources for j in range(2)]
        held = score(*blocks[0], 0)
        for n, block in enumerate(blocks):
            coming = None
            if n + 1 < len(blocks):
                coming = score(*blocks[n + 1], (n + 1) % 2)
            fold(*block, n % 2, *held)
            held = coming

    def send_off(kind):
        m_r, l_r, acc_r = ((m_s, l_s, acc_s), (m_c, l_c, acc_c))[kind]
        dst = (osb, ocb)[kind]
        for i in (2, 1, ny - 1, 0):
            for j in range(2):
                b = 2 * i + j
                cut = slice(j * span, (j + 1) * span)
                total = l_r[b : b + 1, :]
                dst[i, :, cut] = (acc_r[b] / total).astype(BF16)
                stb[kind, i, :, cut] = m_r[b : b + 1, :] * LOG2 + jnp.log2(total)
        for j in range(2):
            o_half(kind, j).start()
        for i in range(1, ny):
            t_copy(kind, i).start()
        for i in (1, ny - 1):
            o_copy(kind, i).start()

    def pass_on(kind):
        for j in range(2):
            o_half(kind, j).wait_recv()
            o_relay(kind, j).start()

    low = (0, 1)
    high = (ny - 1, 2)

    @pl.loop(0, groups)
    def _(g):
        for turn in range(4):
            serve(2 * g + 1 + turn // 2, turn % 2)
            kind = turn // 2
            sources = (low, high)[turn % 2]
            if turn == 3:
                @pl.when(g == 0)
                def _():
                    q_wait(0, ny - 1)
                    q_relay(0).start()

            if turn == 1:
                @pl.when(g == 1)
                def _():
                    q_wait(1, 1)
                    q_relay(1).start()

            @pl.when(g == kind + 1)
            def _():
                for i in sources:
                    if i != (ny - 1, 1)[kind]:
                        q_wait(kind, i)

            @pl.when(g > kind)
            def _():
                attend(kind, g - 1 - kind, sources)

    attend(0, groups - 1, low + high)
    send_off(0)
    attend(1, groups - 2, low + high)
    pass_on(0)
    attend(1, groups - 1, low + high)
    send_off(1)

    for kind in range(2):
        mine, other = ((osb, rsb), (ocb, rcb))[kind]
        final, out = ((fsb, out_s), (fcb, out_c))[kind]
        for i in range(1, ny):
            t_copy(kind, ny - i).wait_recv()
        levels = [stb[kind, 0]] + [rst[kind, i] for i in range(1, ny)]
        top = levels[0]
        for level in levels[1:]:
            top = jnp.maximum(top, level)
        shares = [jnp.exp2(level - top) for level in levels]
        whole = shares[0]
        for share in shares[1:]:
            whole = whole + share
        shares = [share / whole for share in shares]
        for i in (1, ny - 1):
            o_copy(kind, ny - i).wait_recv()
        for j in range(2):
            o_relay(kind, j).wait_recv()
        for pair in range(heads // 2):
            cut = slice(pair * 2 * rows, (pair + 1) * 2 * rows)
            mixed = mine[0, :, cut].astype(F32) * shares[0][:, cut]
            for i in range(1, ny):
                mixed = mixed + other[i, :, cut].astype(F32) * shares[i][:, cut]
            mixed = jnp.transpose(mixed)
            for k in range(2):
                h = 2 * pair + k
                block = mixed[k * rows : (k + 1) * rows, :]
                if kind == 1:
                    block = block * gate[...]
                final[:, :, h * HD : (h + 1) * HD] = block.reshape(
                    nh, rows // nh, HD
                ).astype(BF16)
        for i in range(1, nh):
            f_copy(kind, i).start()
        if kind == 0:
            pass_on(1)
        pltpu.make_async_copy(
            final.at[head],
            out.at[:, pl.ds(pl.multiple_of(head * wide, wide), wide)],
            loc.at[3 + kind],
        ).start()
    for kind in range(2):
        final, out = ((fsb, out_s), (fcb, out_c))[kind]
        for i in range(1, nh):
            f_in(kind, i).wait_recv()
        pltpu.make_async_copy(
            final.at[head],
            out.at[:, pl.ds(pl.multiple_of(head * wide, wide), wide)],
            loc.at[3 + kind],
        ).wait()

    for piece in range(2):
        ring(0, 1, piece, True).wait_send()
        ring(1, 1, piece, True).wait_send()
        ring(0, half, piece).wait_send()

    @pl.loop(2, half)
    def _(d):
        for flow in range(2):
            for piece in range(2):
                ring(flow, d, piece).wait_send()

    for kind in range(2):
        for i in (1, ny - 1):
            q_copy(kind, i).wait_send()
            o_copy(kind, i).wait_send()
        q_relay(kind).wait_send()
        for i in range(1, ny):
            t_copy(kind, i).wait_send()
        for j in range(2):
            o_half(kind, j).wait_send()
            o_relay(kind, j).wait_send()
    for kind in range(2):
        for i in range(1, nh):
            f_copy(kind, i).wait_send()


def on_device(
    nctx, nh,
    query_self, key_self, value_self, positions,
    query_cross, key_vision, value_vision, media_range, gate_scale,
):
    rows, wide = query_self.shape
    real = key_vision.shape[0]
    ny = NY
    nz = nctx // ny
    heads = wide // HD
    zpf = FRAME_LEN // (real * ny)

    exponents = jnp.arange(HD // 2, dtype=F32) * (2.0 / HD)
    frequency = jnp.power(ROPE_BASE, -exponents)
    angles = positions.astype(F32)[:, None] * jnp.tile(frequency, 2)[None, :]
    first = jnp.arange(HD)[None, :] < HD // 2
    cosine = jnp.cos(angles)
    sine = jnp.where(first, -jnp.sin(angles), jnp.sin(angles))

    lower = jnp.repeat(media_range[:, 0], TBLOCK)[:, None]
    upper = jnp.repeat(media_range[:, 1], TBLOCK)[:, None]
    lanes = jnp.arange(HD, dtype=jnp.int32)[None, :]
    hidden = jnp.logical_or(lanes < lower, lanes >= upper)
    hidden = jnp.logical_and(hidden, lanes < nz // zpf)
    hidden = jnp.logical_or(hidden, lanes == HD - 1)
    extra = jnp.where(hidden, -BIG, 0.0).astype(BF16)
    gate = jnp.where(upper > lower, jnp.tanh(gate_scale[0]), 0.0)
    gate = jnp.broadcast_to(gate, (rows, HD)).astype(F32)

    vmem = pl.BlockSpec(memory_space=pltpu.VMEM)
    anywhere = pl.BlockSpec(memory_space=pl.ANY)
    qs, qc, kv = pl.pallas_call(
        prepare_kernel,
        out_shape=(
            jax.ShapeDtypeStruct((rows, wide), BF16),
            jax.ShapeDtypeStruct((rows, wide + HD), BF16),
            jax.ShapeDtypeStruct((2 * rows, 2 * HD), BF16),
        ),
        grid=(1,),
        in_specs=[vmem] * 9,
        out_specs=(
            pl.BlockSpec((rows, wide), lambda g: (0, 0)),
            pl.BlockSpec((rows, wide + HD), lambda g: (0, 0)),
            pl.BlockSpec((2 * rows, 2 * HD), lambda g: (0, 0)),
        ),
        name="prepare",
    )(query_self, key_self, value_self, query_cross, key_vision, value_vision, cosine, sine, extra)

    span = heads // 2 * rows
    row = pltpu.VMEM((2 * ny, span), F32)
    state = pltpu.VMEM((2 * ny, HD, span), F32)
    part = pltpu.VMEM((ny, HD, heads * rows), BF16)
    stat = pltpu.VMEM((2, ny, 1, heads * rows), F32)
    final = pltpu.VMEM((nh, rows // nh, wide), BF16)
    dma = pltpu.SemaphoreType.DMA
    half = nz // 2
    return pl.pallas_call(
        functools.partial(main_kernel, nz, ny, nh, real, zpf),
        out_shape=(jax.ShapeDtypeStruct((rows // nh, wide * nh), BF16),) * 2,
        in_specs=[anywhere] * 3 + [vmem],
        out_specs=(vmem,) * 2,
        scratch_shapes=[
            pltpu.VMEM((nz, 2 * rows, 2 * HD), BF16),
            pltpu.VMEM((ny, rows, wide), BF16),
            pltpu.VMEM((ny, rows, wide + HD), BF16),
            pltpu.VMEM((ny, rows, HD), BF16),
            row, row, state, row, row, state,
            pltpu.VMEM((2, 4 * rows, span), F32),
            pltpu.VMEM((2, 2, HD, span), BF16),
            part, part, stat, part, part, stat, final, final,
            dma((2, half + 1, 2)), dma((2, half + 1, 2)),
            dma((2, ny)), dma((2, ny)),
            dma((4, ny)), dma((4, ny)),
            dma((2, 4)), dma((2, 4)),
            dma((2, nh)), dma((2, nh)),
            dma((5,)),
        ],
        compiler_params=pltpu.CompilerParams(collective_id=0, has_side_effects=True),
        name="attend",
    )(qs, qc, kv, gate)


def solution(mesh):
    placed = (
        P("ctx", "head"),
        P("ctx", "head"),
        P("ctx", "head"),
        P("ctx"),
        P("ctx", "head"),
        P("ctx", "head"),
        P("ctx", "head"),
        P("ctx", None),
        P(),
    )
    body = functools.partial(on_device, mesh.shape["ctx"], mesh.shape["head"])
    return jax.shard_map(
        body,
        mesh=mesh,
        in_specs=placed,
        out_specs=(P(("ctx", "head"), None), P(("ctx", "head"), None)),
        check_vma=False,
    )
```

time: 113 us -> 106 us (0.938)
  Pallas kernels: 104 us -> 97.8 us
    pallas_call x1, Pallas kernels: 102 us -> 96 us  [on_device(): pl.pallas_call(functools.partial(main_kernel, nz, ny, nh, real, zpf), out...]
    unnamed x12 -> x8, local copies, waits for them, and re-layouts: 5.29 us -> 3.59 us
where the time goes in v2:
time: 106 us; the launch traced here: 105 us
  Pallas kernels  97.8 us (92%)
  local copies, waits for them, and re-layouts  4.67 us (4%)
  other arithmetic  1.54 us (1%)
  between operations  1.35 us (1%)
    pallas_call x1, Pallas kernels, on_device(): pl.pallas_call(functools.partial(main_kernel, nz, ny, nh, real, zpf), out...  96 us
    unnamed x8, local copies, waits for them, and re-layouts  3.59 us

profile of v2, /device:TPU:1, one launch (start us, length us, event | category | flops | bytes accessed | tf_op | source)
XLA Modules:
  0.0 105.4 jit_solution(6649154064404831068)
XLA Ops:
  1.3 0.0 copy-start.2
  1.3 0.6 copy-done.2
  2.0 0.1 mul.28
  2.1 0.0 copy-start.1
  2.1 0.7 copy-done.1
  2.8 0.1 broadcast_in_dim.39
  2.8 0.1 lt.42
  2.9 0.1 broadcast_in_dim.40
  3.0 0.1 ge.6
  3.1 0.7 select_convert_fusion.qa
  3.8 0.7 broadcast_in_dim.45.gate
  4.5 0.8 negate_select_fusion
  5.3 1.8 %prepare.1 = (bf16[64,1024]{1,0:T(8,128)(2,1)}, bf16[64,1152]{1,0:T(8,128)(2,1)}, bf16[128,256]{1,0:T(8,128)(2,1)}) custom-call(bf16[64,1024]{1,0:T(8,128)(2,1)} %qs.1, bf16[64,128]{1,0:T(8,128)(2,1)} %ks.1, bf16[64,128]{1,0:T(8,128)(2,1)} %vs.1, bf16[64,1024]{1,0:T(8,128)(2,1)} %qc.1, bf16[56,128]{1,0:T(8,128)(2,1)} %kf.1, bf16[56,128]{1,0:T(8,128)(2,1)} %vf.1, ...), custom_call_target="tpu_custom_call" | custom-call | tf_op jit(solution)/shard_map/prepare/pallas_call | solution.py:485
  7.1 96.0 %attend.1 = (bf16[8,8192]{1,0:T(8,128)(2,1)}, bf16[8,8192]{1,0:T(8,128)(2,1)}) custom-call(bf16[64,1024]{1,0:T(8,128)(2,1)} %get-tuple-element.5.qs, bf16[64,1152]{1,0:T(8,128)(2,1)} %get-tuple-element.6.qc, bf16[128,256]{1,0:T(8,128)(2,1)} %get-tuple-element.7.kv, f32[64,128]{1,0:T(8,128)} %broadcast_in_dim.45.gate), custom_call_target="tpu_custom_call" | custom-call | tf_op jit(solution)/shard_map/attend/pallas_call | solution.py:510
  103.1 0.0 copy-start
  103.1 1.6 %copy.14 = bf16[8,8192]{1,0:T(8,128)(2,1)} copy(bf16[8,8192]{1,0:T(8,128)(2,1)} %get-tuple-element.16) | data formatting | bytes 262144
  104.7 0.0 copy-done
  104.7 0.7 copy.15
  (7 shorter events, 0.0 us)
Async XLA Ops:
  1.3 0.7 copy-start.2
  2.1 0.7 copy-start.1
  103.1 1.6 %copy-start = (bf16[8,8192]{1,0:T(8,128)(2,1)S(1)}, bf16[8,8192]{1,0:T(8,128)(2,1)}, u32[]{:S(2)}) copy-start(bf16[8,8192]{1,0:T(8,128)(2,1)} %get-tuple-element.17) | copy-start | bytes 393220

commit v3 on v2

--- a/solution.py
+++ b/solution.py
@@ -56,7 +56,7 @@
     packed = heads // 2
     span = packed * rows
     half = nz // 2
-    groups = nz // 4
+    lag = 5
     ctx = lax.axis_index("ctx")
     head = lax.axis_index("head")
     z = ctx // ny
@@ -231,23 +231,37 @@
     own_qs.wait()
     own_qc.wait()
 
-    def serve(d, piece):
-        ring_in(0, d, piece).wait_recv()
-
-        @pl.when(d < half)
-        def _():
-            ring(0, d + 1, piece).start()
-
-        @pl.when(d < half)
-        def _():
-            ring_in(1, d, piece).wait_recv()
+    def serve_up(d, piece):
+        ring_in(1, d, piece).wait_recv()
 
         @pl.when(d < half - 1)
         def _():
             ring(1, d + 1, piece).start()
 
+    def serve(step, piece):
+        @pl.when(step <= half)
+        def _():
+            ring_in(0, step, piece).wait_recv()
+
+        @pl.when(step < half)
+        def _():
+            ring(0, step + 1, piece).start()
+
+        @pl.when(jnp.logical_and(step <= z, step < half))
+        def _():
+            serve_up(step, piece)
+
+        late_step = step - lag
+
+        @pl.when(
+            jnp.logical_and(late_step > z, jnp.logical_and(late_step >= 1, late_step < half))
+        )
+        def _():
+            serve_up(late_step, piece)
+
     def keys_of(kind, group):
-        offsets = (-2 * group, -2 * group - 1, 2 * group + 1, 2 * group + 2)
+        upper, j = group
+        offsets = [jnp.where(upper, 4 * j + 1 + r, -4 * j - r) for r in range(4)]
         keys, marks, values = [], [], []
         lanes = lax.broadcasted_iota(jnp.int32, (rows, HD), 1)
         index = lax.broadcasted_iota(jnp.int32, (rows, HD), 0)
@@ -339,39 +353,43 @@
     low = (0, 1)
     high = (ny - 1, 2)
 
-    @pl.loop(0, groups)
-    def _(g):
-        for turn in range(4):
-            serve(2 * g + 1 + turn // 2, turn % 2)
-            kind = turn // 2
-            sources = (low, high)[turn % 2]
-            if turn == 3:
-                @pl.when(g == 0)
+    @pl.loop(1, half + lag)
+    def _(step):
+        early = step < 9
+        place = jnp.maximum(step - 9, 0) // 2
+        upper = jnp.logical_or(early, place % 2 == 0)
+        j = jnp.where(early, 0, jnp.where(upper, place // 2 + 1, place // 2))
+        busy = jnp.logical_or(step >= 9, jnp.logical_or(step == 5, step == 6))
+        for piece in range(2):
+            serve(step, piece)
+            sources = (low, high)[piece]
+            if piece == 1:
+                @pl.when(step == 2)
                 def _():
                     q_wait(0, ny - 1)
                     q_relay(0).start()
 
-            if turn == 1:
-                @pl.when(g == 1)
+                @pl.when(step == 3)
                 def _():
                     q_wait(1, 1)
                     q_relay(1).start()
 
-            @pl.when(g == kind + 1)
-            def _():
-                for i in sources:
-                    if i != (ny - 1, 1)[kind]:
-                        q_wait(kind, i)
-
-            @pl.when(g > kind)
-            def _():
-                attend(kind, g - 1 - kind, sources)
-
-    attend(0, groups - 1, low + high)
+            for kind in range(2):
+                @pl.when(step == 5 + kind)
+                def _():
+                    for i in sources:
+                        if i != (ny - 1, 1)[kind]:
+                            q_wait(kind, i)
+
+                @pl.when(jnp.logical_and(busy, step % 2 == 1 - kind))
+                def _():
+                    attend(kind, (upper, j), sources)
+
+    last_group = (False, nz // 8 - 1)
+    attend(0, last_group, low + high)
     send_off(0)
-    attend(1, groups - 2, low + high)
+    attend(1, last_group, low + high)
     pass_on(0)
-    attend(1, groups - 1, low + high)
     send_off(1)
 
     for kind in range(2):

time: 106 us -> 113 us (1.066); the launches traced: 105 us -> 110 us
  Pallas kernels: 97.8 us -> 103 us
    pallas_call x1, Pallas kernels: 96 us -> 101 us  [on_device(): pl.pallas_call(functools.partial(main_kernel, nz, ny, nh, real, zpf), out...]
where the time goes in v3:
time: 113 us; the launch traced here: 110 us
  Pallas kernels  103 us (91%)
  local copies, waits for them, and re-layouts  4.67 us (4%)
  other arithmetic  1.54 us (1%)
  between operations  1.35 us (1%)
    pallas_call x1, Pallas kernels, on_device(): pl.pallas_call(functools.partial(main_kernel, nz, ny, nh, real, zpf), out...  101 us
    unnamed x8, local copies, waits for them, and re-layouts  3.59 us

profile of v3, /device:TPU:1, one launch (start us, length us, event | category | flops | bytes accessed | tf_op | source)
XLA Modules:
  0.0 110.5 jit_solution(9201804082988436224)
XLA Ops:
  1.3 0.0 copy-start.2
  1.3 0.6 copy-done.2
  2.0 0.1 mul.28
  2.1 0.0 copy-start.1
  2.1 0.7 copy-done.1
  2.8 0.1 broadcast_in_dim.39
  2.8 0.1 lt.42
  2.9 0.1 broadcast_in_dim.40
  3.0 0.1 ge.6
  3.1 0.7 select_convert_fusion.qa
  3.8 0.7 broadcast_in_dim.45.gate
  4.5 0.8 negate_select_fusion
  5.3 1.8 %prepare.1 = (bf16[64,1024]{1,0:T(8,128)(2,1)}, bf16[64,1152]{1,0:T(8,128)(2,1)}, bf16[128,256]{1,0:T(8,128)(2,1)}) custom-call(bf16[64,1024]{1,0:T(8,128)(2,1)} %qs.1, bf16[64,128]{1,0:T(8,128)(2,1)} %ks.1, bf16[64,128]{1,0:T(8,128)(2,1)} %vs.1, bf16[64,1024]{1,0:T(8,128)(2,1)} %qc.1, bf16[56,128]{1,0:T(8,128)(2,1)} %kf.1, bf16[56,128]{1,0:T(8,128)(2,1)} %vf.1, ...), custom_call_target="tpu_custom_call" | custom-call | tf_op jit(solution)/shard_map/prepare/pallas_call | solution.py:503
  7.1 101.1 %attend.1 = (bf16[8,8192]{1,0:T(8,128)(2,1)}, bf16[8,8192]{1,0:T(8,128)(2,1)}) custom-call(bf16[64,1024]{1,0:T(8,128)(2,1)} %get-tuple-element.5.qs, bf16[64,1152]{1,0:T(8,128)(2,1)} %get-tuple-element.6.qc, bf16[128,256]{1,0:T(8,128)(2,1)} %get-tuple-element.7.kv, f32[64,128]{1,0:T(8,128)} %broadcast_in_dim.45.gate), custom_call_target="tpu_custom_call" | custom-call | tf_op jit(solution)/shard_map/attend/pallas_call | solution.py:528
  108.2 0.0 copy-start
  108.2 1.6 %copy.14 = bf16[8,8192]{1,0:T(8,128)(2,1)} copy(bf16[8,8192]{1,0:T(8,128)(2,1)} %get-tuple-element.16) | data formatting | bytes 262144
  109.8 0.0 copy-done
  109.8 0.7 copy.15
  (7 shorter events, 0.0 us)
Async XLA Ops:
  1.3 0.7 copy-start.2
  2.1 0.7 copy-start.1
  108.2 1.6 %copy-start = (bf16[8,8192]{1,0:T(8,128)(2,1)S(1)}, bf16[8,8192]{1,0:T(8,128)(2,1)}, u32[]{:S(2)}) copy-start(bf16[8,8192]{1,0:T(8,128)(2,1)} %get-tuple-element.17) | copy-start | bytes 393220

commit v4 on v2

--- a/solution.py
+++ b/solution.py
@@ -363,15 +363,21 @@
                     if i != (ny - 1, 1)[kind]:
                         q_wait(kind, i)
 
+            behind = 1 if kind == 0 else jnp.where(g > 4, 1, 2)
+
             @pl.when(g > kind)
             def _():
-                attend(kind, g - 1 - kind, sources)
+                attend(kind, g - behind, sources)
+
+            if kind == 1:
+                @pl.when(g == 4)
+                def _():
+                    attend(kind, g - 1, sources)
 
     attend(0, groups - 1, low + high)
     send_off(0)
-    attend(1, groups - 2, low + high)
+    attend(1, groups - 1, low + high)
     pass_on(0)
-    attend(1, groups - 1, low + high)
     send_off(1)
 
     for kind in range(2):

time: 106 us -> 106 us (level)
  no operation moved by 1% of the time
where the time goes in v4:
time: 106 us
  Pallas kernels  98.4 us (93%)
  local copies, waits for them, and re-layouts  4.67 us (4%)
  other arithmetic  1.54 us (1%)
  between operations  1.35 us (1%)
    pallas_call x1, Pallas kernels, on_device(): pl.pallas_call(functools.partial(main_kernel, nz, ny, nh, real, zpf), out...  96.6 us
    unnamed x8, local copies, waits for them, and re-layouts  3.59 us

profile of v4, /device:TPU:1, one launch (start us, length us, event | category | flops | bytes accessed | tf_op | source)
XLA Modules:
  0.0 105.9 jit_solution(14351231413128445421)
XLA Ops:
  1.3 0.0 copy-start.2
  1.3 0.6 copy-done.2
  2.0 0.1 mul.28
  2.1 0.0 copy-start.1
  2.1 0.7 copy-done.1
  2.8 0.1 broadcast_in_dim.39
  2.8 0.1 lt.42
  2.9 0.1 broadcast_in_dim.40
  3.0 0.1 ge.6
  3.1 0.7 select_convert_fusion.qa
  3.8 0.7 broadcast_in_dim.45.gate
  4.5 0.8 negate_select_fusion
  5.3 1.8 %prepare.1 = (bf16[64,1024]{1,0:T(8,128)(2,1)}, bf16[64,1152]{1,0:T(8,128)(2,1)}, bf16[128,256]{1,0:T(8,128)(2,1)}) custom-call(bf16[64,1024]{1,0:T(8,128)(2,1)} %qs.1, bf16[64,128]{1,0:T(8,128)(2,1)} %ks.1, bf16[64,128]{1,0:T(8,128)(2,1)} %vs.1, bf16[64,1024]{1,0:T(8,128)(2,1)} %qc.1, bf16[56,128]{1,0:T(8,128)(2,1)} %kf.1, bf16[56,128]{1,0:T(8,128)(2,1)} %vf.1, ...), custom_call_target="tpu_custom_call" | custom-call | tf_op jit(solution)/shard_map/prepare/pallas_call | solution.py:491
  7.1 96.6 %attend.1 = (bf16[8,8192]{1,0:T(8,128)(2,1)}, bf16[8,8192]{1,0:T(8,128)(2,1)}) custom-call(bf16[64,1024]{1,0:T(8,128)(2,1)} %get-tuple-element.5.qs, bf16[64,1152]{1,0:T(8,128)(2,1)} %get-tuple-element.6.qc, bf16[128,256]{1,0:T(8,128)(2,1)} %get-tuple-element.7.kv, f32[64,128]{1,0:T(8,128)} %broadcast_in_dim.45.gate), custom_call_target="tpu_custom_call" | custom-call | tf_op jit(solution)/shard_map/attend/pallas_call | solution.py:516
  103.7 0.0 copy-start
  103.7 1.6 %copy.14 = bf16[8,8192]{1,0:T(8,128)(2,1)} copy(bf16[8,8192]{1,0:T(8,128)(2,1)} %get-tuple-element.16) | data formatting | bytes 262144
  105.3 0.0 copy-done
  105.3 0.7 copy.15
  (7 shorter events, 0.0 us)
Async XLA Ops:
  1.3 0.7 copy-start.2
  2.1 0.7 copy-start.1
  103.7 1.6 %copy-start = (bf16[8,8192]{1,0:T(8,128)(2,1)S(1)}, bf16[8,8192]{1,0:T(8,128)(2,1)}, u32[]{:S(2)}) copy-start(bf16[8,8192]{1,0:T(8,128)(2,1)} %get-tuple-element.17) | copy-start | bytes 393220
